TPU v7x, 128 devices: a whole 4x4x4 slice. The times are simulated.
128 devices in a mesh: row: 32 (over z, y, core), col: 4 (over x).
Axes of the slice: x: 4, y: 4, z: 4, core: 2. Of those that a mesh axis runs over, the one named last changes fastest.
Arguments:
- tokens: bfloat16 [16384, 2048], P('row', 'col'), may hold values from -6 to 6
- cotangent: bfloat16 [16384, 2048], P('row', 'col'), may hold values from -6 to 6
- destination: int32 [16384], P('row'), may hold values from 0 to 16383, as said below
- segment_ids: int32 [16384], P('row'), may hold values from 0 to 7, as said below
- attn_gain: float32 [2048], replicated, may hold values from 0.5 to 1.5
- w_query: bfloat16 [2048, 2048], P('row', 'col'), may hold values from -0.125 to 0.125
- w_key: bfloat16 [2048, 256], P('row', 'col'), may hold values from -0.125 to 0.125
- w_value: bfloat16 [2048, 256], P('row', 'col'), may hold values from -0.125 to 0.125
- w_output: bfloat16 [2048, 2048], P('row', 'col'), may hold values from -0.5 to 0.5
- ffn_gain: float32 [2048], replicated, may hold values from 0.5 to 1.5
- w_gate: bfloat16 [2048, 5632], P('row', 'col'), may hold values from -0.125 to 0.125
- w_up: bfloat16 [2048, 5632], P('row', 'col'), may hold values from -0.125 to 0.125
- w_down: bfloat16 [2048, 5632], P('row', 'col'), may hold values from -0.078125 to 0.078125
Outputs:
- output: bfloat16 [16384, 2048], P('row', 'col')
- input_grad: bfloat16 [16384, 2048], P('row', 'col')
- attn_gain_grad: float32 [2048], P('row')
- w_query_grad: float32 [2048, 2048], P('row', 'col')
- w_key_grad: float32 [2048, 256], P('row', 'col')
- w_value_grad: float32 [2048, 256], P('row', 'col')
- w_output_grad: float32 [2048, 2048], P('row', 'col')
- ffn_gain_grad: float32 [2048], P('row')
- w_gate_grad: float32 [2048, 5632], P('row', 'col')
- w_up_grad: float32 [2048, 5632], P('row', 'col')
- w_down_grad: float32 [2048, 5632], P('row', 'col')
Inputs may be any that keep to these rules, and one draw needn't show every extreme that they name: `destination`: A permutation; the tokens of each aligned block of 512 arriving tokens go to exactly 16 places in each aligned block of 512 balanced places. `segment_ids`: within each aligned block of 512 places the ids start at 0 and rise by one where a new sequence begins, so a block holds at most 8 sequences; in every draw some block holds a single sequence of 512 tokens and some block holds 8 sequences.
All inputs are finite; a program needn't handle non-finite values.
Results may differ from a plain program's by a relative error of at most 0.028.
Values may be sent and summed in bfloat16 or wider, within the bound.
No kernel may reach another device: no remote copies, remote signals or barrier semaphores. Data moves between devices by JAX's collectives and lax.ppermute only.
A program may use at most 128 MiB of HBM per device.

v0:
```python
from functools import partial
import jax
import jax.numpy as jnp
from jax import lax
from jax.sharding import PartitionSpec as P

HEADS = 32
KV = 4
HD = 64
EPS = 1e-05
ROPE_BASE = 10000.0


def rope_tables(positions):
    half_width = HD // 2
    freqs = ROPE_BASE ** (-(jnp.arange(half_width, dtype=jnp.float32) * 2.0 / HD))
    angles = positions.astype(jnp.float32)[:, None] * freqs[None, :]
    return (jnp.cos(angles)[:, None, :], jnp.sin(angles)[:, None, :])


def rotate(values, cosine, sine):
    half_width = values.shape[-1] // 2
    first = values[..., :half_width]
    second = values[..., half_width:]
    return jnp.concatenate(
        [first * cosine - second * sine, second * cosine + first * sine], axis=-1
    )


def rotate_back(grads, cosine, sine):
    half_width = grads.shape[-1] // 2
    first = grads[..., :half_width]
    second = grads[..., half_width:]
    return jnp.concatenate(
        [first * cosine + second * sine, second * cosine - first * sine], axis=-1
    )


def positions_of(segment_ids):
    index = jnp.arange(segment_ids.shape[0], dtype=jnp.int32)
    change = jnp.concatenate([jnp.ones((1,), dtype=jnp.bool_), segment_ids[1:] != segment_ids[:-1]])
    starts = jnp.where(change, index, jnp.zeros_like(index))
    return index - lax.cummax(starts, axis=0)


def allowed_pairs(segment_ids):
    index = jnp.arange(segment_ids.shape[0], dtype=jnp.int32)
    return (segment_ids[:, None] == segment_ids[None, :]) & (index[None, :] <= index[:, None])


def rms_scale(values):
    return lax.rsqrt(jnp.mean(values * values, axis=-1, keepdims=True) + EPS)


def norm_back(values, inv_root, gain, grads):
    normed = values * inv_root
    scaled = grads * gain
    result = inv_root * (scaled - normed * jnp.mean(scaled * normed, axis=-1, keepdims=True))
    return (result, jnp.sum(grads * normed, axis=0))


def matmul(left, right):
    return jnp.dot(left, right, preferred_element_type=jnp.float32)


def head_scores(query_head, key_head, allowed, scale_factor):
    scores = matmul(query_head, key_head.T) * scale_factor
    return jnp.where(allowed, scores, -1e30)


def head_forward(inputs, key_heads, value_heads, allowed, scale_factor):
    query_head, kv_slot = inputs
    scores = head_scores(query_head, key_heads[kv_slot], allowed, scale_factor)
    peak = jnp.max(scores, axis=-1, keepdims=True)
    expo = jnp.exp(scores - peak)
    total = jnp.sum(expo, axis=-1, keepdims=True)
    probs = expo / total
    mixed = matmul(probs.astype(jnp.bfloat16), value_heads[kv_slot])
    return (mixed, (peak + jnp.log(total))[:, 0])


def head_backward(inputs, key_heads, value_heads, allowed, scale_factor):
    query_head, kv_slot, grad_head, log_total = inputs
    key_head = key_heads[kv_slot]
    value_head = value_heads[kv_slot]
    scores = head_scores(query_head, key_head, allowed, scale_factor)
    probs = jnp.exp(scores - log_total[:, None])
    prob_grad = matmul(grad_head, value_head.T)
    value_grad = matmul(probs.astype(jnp.bfloat16).T, grad_head)
    inner = jnp.sum(probs * prob_grad, axis=-1, keepdims=True)
    score_grad = (probs * (prob_grad - inner)).astype(jnp.bfloat16)
    query_grad = matmul(score_grad, key_head) * scale_factor
    key_grad = matmul(score_grad.T, query_head) * scale_factor
    return (query_grad, key_grad, value_grad)


def body(
    tokens,
    cotangent,
    destination,
    segment_ids,
    attn_gain,
    w_query,
    w_key,
    w_value,
    w_output,
    ffn_gain,
    w_gate,
    w_up,
    w_down,
):
    row_count = tokens.shape[0]
    quarter = tokens.shape[1]
    col_start = lax.axis_index("col") * quarter
    group_size = HEADS // KV
    send_order = jnp.argsort(destination)
    slot_ids = destination[send_order] % row_count
    arrived_rows, arrived_grads, arrived_slots = (
        lax.all_to_all(tokens[send_order], "row", split_axis=0, concat_axis=0, tiled=True),
        lax.all_to_all(cotangent[send_order], "row", split_axis=0, concat_axis=0, tiled=True),
        lax.all_to_all(slot_ids, "row", split_axis=0, concat_axis=0, tiled=True),
    )
    placing = jnp.argsort(arrived_slots)
    full_rows, full_grads = (
        lax.all_gather(arrived_rows[placing], "col", axis=1, tiled=True),
        lax.all_gather(arrived_grads[placing], "col", axis=1, tiled=True),
    )
    query_w, key_w, value_w, output_w = (
        lax.all_gather(w_query, "row", axis=0, tiled=True),
        lax.all_gather(w_key, "row", axis=0, tiled=True),
        lax.all_gather(w_value, "row", axis=0, tiled=True),
        lax.all_gather(w_output, "row", axis=0, tiled=True),
    )
    cosine, sine = rope_tables(positions_of(segment_ids))
    allowed = allowed_pairs(segment_ids)
    rows_wide = full_rows.astype(jnp.float32)
    inv_one = rms_scale(rows_wide)
    normed_one = (rows_wide * inv_one * attn_gain).astype(jnp.bfloat16)
    query = matmul(normed_one, query_w)
    key_raw = matmul(normed_one, key_w)
    value_raw = matmul(normed_one, value_w)
    query_heads_count = query.shape[1] // HD
    kv_count = key_raw.shape[1] // HD
    query_rot = (
        rotate(query.reshape(row_count, query_heads_count, HD), cosine, sine)
        .astype(jnp.bfloat16)
        .transpose(1, 0, 2)
    )
    key_rot = (
        rotate(key_raw.reshape(row_count, kv_count, HD), cosine, sine)
        .astype(jnp.bfloat16)
        .transpose(1, 0, 2)
    )
    value_heads = value_raw.astype(jnp.bfloat16).reshape(row_count, kv_count, HD).transpose(1, 0, 2)
    kv_slots = jnp.arange(query_heads_count, dtype=jnp.int32) // group_size
    scale_factor = HD ** (-0.5)
    mixed_heads, log_totals = lax.map(
        partial(
            head_forward,
            key_heads=key_rot,
            value_heads=value_heads,
            allowed=allowed,
            scale_factor=scale_factor,
        ),
        (query_rot, kv_slots),
    )
    mixed = (
        mixed_heads.transpose(1, 0, 2)
        .reshape(row_count, query_heads_count * HD)
        .astype(jnp.bfloat16)
    )
    attn_terms = matmul(mixed, output_w.T)
    attn_full = lax.psum(attn_terms, "col")
    resid = rows_wide + attn_full
    inv_two = rms_scale(resid)
    normed_two = (resid * inv_two * ffn_gain).astype(jnp.bfloat16)
    resid_part = lax.dynamic_slice_in_dim(resid, col_start, quarter, 1)
    gate_w, up_w, down_w = (
        lax.all_gather(w_gate, "row", axis=0, tiled=True),
        lax.all_gather(w_up, "row", axis=0, tiled=True),
        lax.all_gather(w_down, "row", axis=0, tiled=True),
    )
    gate = matmul(normed_two, gate_w)
    upper = matmul(normed_two, up_w)
    sigmoid_gate = jax.nn.sigmoid(gate)
    activ = (gate * sigmoid_gate * upper).astype(jnp.bfloat16)
    ffn_share = lax.psum_scatter(
        matmul(activ, down_w.T).astype(jnp.bfloat16), "col", scatter_dimension=1, tiled=True
    ).astype(jnp.float32)
    output_share = (resid_part + ffn_share).astype(jnp.bfloat16)
    gate_w, up_w, down_w = (
        lax.all_gather(w_gate, "row", axis=0, tiled=True),
        lax.all_gather(w_up, "row", axis=0, tiled=True),
        lax.all_gather(w_down, "row", axis=0, tiled=True),
    )
    down_weight_grad = matmul(full_grads.T, activ)
    act_grad = matmul(full_grads, down_w)
    gate_grad = (act_grad * upper * sigmoid_gate * (1.0 + gate * (1.0 - sigmoid_gate))).astype(
        jnp.bfloat16
    )
    up_grad = (act_grad * gate * sigmoid_gate).astype(jnp.bfloat16)
    gate_weight_grad = matmul(normed_two.T, gate_grad)
    up_weight_grad = matmul(normed_two.T, up_grad)
    normed_terms_two = matmul(gate_grad, gate_w.T) + matmul(up_grad, up_w.T)
    normed_grad_two = lax.psum(normed_terms_two, "col")
    resid_norm_grad, ffn_gain_grad = norm_back(resid, inv_two, ffn_gain, normed_grad_two)
    resid_grad = full_grads.astype(jnp.float32) + resid_norm_grad
    attn_grad_low = resid_grad.astype(jnp.bfloat16)
    ffn_results = (
        lax.psum_scatter(
            gate_weight_grad.astype(jnp.bfloat16), "row", scatter_dimension=0, tiled=True
        ).astype(jnp.float32),
        lax.psum_scatter(
            up_weight_grad.astype(jnp.bfloat16), "row", scatter_dimension=0, tiled=True
        ).astype(jnp.float32),
        lax.psum_scatter(
            down_weight_grad.astype(jnp.bfloat16), "row", scatter_dimension=0, tiled=True
        ).astype(jnp.float32),
        lax.psum_scatter(
            ffn_gain_grad.astype(jnp.bfloat16), "row", scatter_dimension=0, tiled=True
        ).astype(jnp.float32),
    )
    query_w, key_w, value_w, output_w = (
        lax.all_gather(w_query, "row", axis=0, tiled=True),
        lax.all_gather(w_key, "row", axis=0, tiled=True),
        lax.all_gather(w_value, "row", axis=0, tiled=True),
        lax.all_gather(w_output, "row", axis=0, tiled=True),
    )
    output_weight_grad = matmul(attn_grad_low.T, mixed)
    mixed_grad = matmul(attn_grad_low, output_w).astype(jnp.bfloat16)
    mixed_grad_heads = mixed_grad.reshape(row_count, query_heads_count, HD).transpose(1, 0, 2)
    query_grads, key_grads, value_grads = lax.map(
        partial(
            head_backward,
            key_heads=key_rot,
            value_heads=value_heads,
            allowed=allowed,
            scale_factor=scale_factor,
        ),
        (query_rot, kv_slots, mixed_grad_heads, log_totals),
    )
    query_grad = (
        rotate_back(query_grads.transpose(1, 0, 2), cosine, sine)
        .reshape(row_count, query_heads_count * HD)
        .astype(jnp.bfloat16)
    )
    key_sum = key_grads.reshape(kv_count, group_size, row_count, HD).sum(axis=1).transpose(1, 0, 2)
    key_grad = (
        rotate_back(key_sum, cosine, sine).reshape(row_count, kv_count * HD).astype(jnp.bfloat16)
    )
    value_sum = (
        value_grads.reshape(kv_count, group_size, row_count, HD).sum(axis=1).transpose(1, 0, 2)
    )
    value_grad = value_sum.reshape(row_count, kv_count * HD).astype(jnp.bfloat16)
    query_weight_grad = matmul(normed_one.T, query_grad)
    key_weight_grad = matmul(normed_one.T, key_grad)
    value_weight_grad = matmul(normed_one.T, value_grad)
    normed_terms_one = (
        matmul(query_grad, query_w.T) + matmul(key_grad, key_w.T) + matmul(value_grad, value_w.T)
    )
    normed_grad_one = lax.psum(normed_terms_one.astype(jnp.bfloat16), "col").astype(jnp.float32)
    rows_norm_grad, attn_gain_grad = norm_back(rows_wide, inv_one, attn_gain, normed_grad_one)
    rows_grad = resid_grad + rows_norm_grad
    input_share = lax.dynamic_slice_in_dim(rows_grad, col_start, quarter, 1).astype(jnp.bfloat16)
    attn_results = (
        lax.psum_scatter(
            query_weight_grad.astype(jnp.bfloat16), "row", scatter_dimension=0, tiled=True
        ).astype(jnp.float32),
        lax.psum_scatter(
            key_weight_grad.astype(jnp.bfloat16), "row", scatter_dimension=0, tiled=True
        ).astype(jnp.float32),
        lax.psum_scatter(
            value_weight_grad.astype(jnp.bfloat16), "row", scatter_dimension=0, tiled=True
        ).astype(jnp.float32),
        lax.psum_scatter(
            output_weight_grad.astype(jnp.bfloat16), "row", scatter_dimension=0, tiled=True
        ).astype(jnp.float32),
        lax.psum_scatter(
            attn_gain_grad.astype(jnp.bfloat16), "row", scatter_dimension=0, tiled=True
        ).astype(jnp.float32),
    )
    back_rows, back_grads = (
        lax.all_to_all(output_share[arrived_slots], "row", split_axis=0, concat_axis=0, tiled=True),
        lax.all_to_all(input_share[arrived_slots], "row", split_axis=0, concat_axis=0, tiled=True),
    )
    restore = jnp.argsort(send_order)
    return (
        back_rows[restore],
        back_grads[restore],
        attn_results[4],
        attn_results[0],
        attn_results[1],
        attn_results[2],
        attn_results[3],
        ffn_results[3],
        ffn_results[0],
        ffn_results[1],
        ffn_results[2],
    )


def solution(mesh):
    placed = (
        P("row", "col"),
        P("row", "col"),
        P("row"),
        P("row"),
        P(),
        P("row", "col"),
        P("row", "col"),
        P("row", "col"),
        P("row", "col"),
        P(),
        P("row", "col"),
        P("row", "col"),
        P("row", "col"),
    )
    return jax.shard_map(
        body,
        mesh=mesh,
        in_specs=placed,
        out_specs=(
            P("row", "col"),
            P("row", "col"),
            P("row"),
            P("row", "col"),
            P("row", "col"),
            P("row", "col"),
            P("row", "col"),
            P("row"),
            P("row", "col"),
            P("row", "col"),
            P("row", "col"),
        ),
        check_vma=False,
    )
```

profile of v0, /device:TPU:0, one launch (start us, length us, event | category | flops | bytes accessed | tf_op | source)
XLA Modules:
  0.0 1312.7 jit_solution(15525933860058886407)
XLA Ops:
  7.2 4.5 sort.45
  12.3 3.6 gather_fusion.1
  16.6 8.4 all-to-all-start.1
  27.7 4.6 all-to-all-done.1
  32.3 3.9 all-to-all-start
  37.6 3.8 sort.46
  41.4 6.6 all-to-all-done
  53.0 22.4 %all_gather.36 = bf16[2048,64]{1,0:T(8,128)(2,1)S(1)} all-gather(bf16[64,64]{1,0:T(8,128)(2,1)S(1)} %copy-done.22), channel_id=1, replica_groups=mesh['row'=32,'col'=4] {'row'}, dimensions={0}, use_global_device_ids=true | all-gather | bytes 270336 | tf_op jit(solution)/shard_map/all_gather | solution.py:130
  75.5 26.7 %all_gather.37 = bf16[2048,64]{1,0:T(8,128)(2,1)} all-gather(bf16[64,64]{1,0:T(8,128)(2,1)S(1)} %copy-done.23), channel_id=1, replica_groups=mesh['row'=32,'col'=4] {'row'}, dimensions={0}, use_global_device_ids=true | all-gather | bytes 270336 | tf_op jit(solution)/shard_map/all_gather | solution.py:131
  111.2 14.4 %all-gather.10.cloned.1.call-done = bf16[2048,512]{1,0:T(8,128)(2,1)} async-done(((bf16[64,512]{1,0:T(8,128)(2,1)}), bf16[2048,512]{1,0:T(8,128)(2,1)}) %all-gather.10.cloned.1.call-update) | async-done | bytes 2097168 | tf_op jit(solution)/shard_map/all_gather | solution.py:129
  125.6 3.0 fusion.73
  129.4 24.0 %while.32 = (s32[]{:T(128)}, bf16[8,512,64]{1,2,0:T(8,128)(2,1)S(1)}, f32[8,512]{1,0:T(8,128)}, bf16[8,512,64]{2,1,0:T(8,128)(2,1)S(1)}, bf16[1,512,64]{2,1,0:T(...) while((s32[]{:T(128)}, bf16[8,512,64]{1,2,0:T(8,128)(2,1)S(1)}, ...), condition=%wide.region_8.9_spmd.clone.clone, body=%wide.region_5.8_spmd.clone.sunk.clone | while | flops 69991936 | bytes 3695189 | solution.py:157
  153.4 17.8 %all-gather.12.cloned.1.call-done = bf16[2048,512]{1,0:T(8,128)(2,1)} async-done(((bf16[64,512]{1,0:T(8,128)(2,1)}), bf16[2048,512]{1,0:T(8,128)(2,1)}) %all-gather.12.cloned.1.call-update) | async-done | bytes 2097168 | tf_op jit(solution)/shard_map/all_gather | solution.py:132
  171.2 4.9 fusion.75
  180.0 17.1 %all_to_all.60 = bf16[32,16,512]{2,1,0:T(8,128)(2,1)S(1)} all-to-all(bf16[32,16,512]{2,1,0:T(8,128)(2,1)} %bitcast.194), channel_id=1, replica_groups=mesh['row'=32,'col'=4] {'row'}, dimensions={0} | all-to-all | bytes 1048576 | tf_op jit(solution)/shard_map/all_to_all | solution.py:120
  201.1 67.2 %all-reduce.7.cloned.1.call-done = f32[512,2048]{1,0:T(8,128)} async-done(((f32[512,2048]{1,0:T(8,128)}), f32[512,2048]{1,0:T(8,128)}) %all-reduce.7.cloned.1.call-update) | async-done | bytes 4194320 | tf_op jit(solution)/shard_map/psum | solution.py:173
  268.3 2.8 multiply_reduce_fusion.4
  274.8 44.2 %all-gather.14.cloned.1.call-done = bf16[2048,1408]{1,0:T(8,128)(2,1)} async-done(((bf16[64,1408]{1,0:T(8,128)(2,1)}), bf16[2048,1408]{1,0:T(8,128)(2,1)}) %all-gather.14.cloned.1.call-update) | async-done | bytes 5767184 | tf_op jit(solution)/shard_map/all_gather | solution.py:179
  319.0 8.3 fusion.76
  327.3 41.5 %all-gather.16.cloned.1.call-done = bf16[2048,1408]{1,0:T(8,128)(2,1)} async-done(((bf16[64,1408]{1,0:T(8,128)(2,1)}), bf16[2048,1408]{1,0:T(8,128)(2,1)}) %all-gather.16.cloned.1.call-update) | async-done | bytes 5767184 | tf_op jit(solution)/shard_map/all_gather | solution.py:180
  368.8 8.3 fusion.77
  377.1 23.9 %all-gather.22.cloned.1.call-done = bf16[512,2048]{1,0:T(8,128)(2,1)} async-done(((bf16[512,512]{1,0:T(8,128)(2,1)}), bf16[512,2048]{1,0:T(8,128)(2,1)}) %all-gather.22.cloned.1.call-update) | async-done | bytes 2097168 | tf_op jit(solution)/shard_map/all_gather | solution.py:126
  400.9 51.0 %all-gather.18.cloned.1.call-done = bf16[2048,1408]{1,0:T(8,128)(2,1)} async-done(((bf16[64,1408]{1,0:T(8,128)(2,1)}), bf16[2048,1408]{1,0:T(8,128)(2,1)}) %all-gather.18.cloned.1.call-update) | async-done | bytes 5767184 | tf_op jit(solution)/shard_map/all_gather | solution.py:181
  452.0 10.3 multiply_convert_fusion.3
  462.3 6.6 fusion.78
  468.9 5.1 convolution_add_fusion
  474.2 7.9 convolution_convert_fusion.5
  482.2 83.7 %all-reduce.9.cloned.1.call-done = f32[512,2048]{1,0:T(8,128)} async-done(((f32[512,2048]{1,0:T(8,128)}), f32[512,2048]{1,0:T(8,128)}) %all-reduce.9.cloned.1.call-update) | async-done | bytes 4194320 | tf_op jit(solution)/shard_map/psum | solution.py:205
  565.9 5.2 multiply_reduce_fusion.1
  571.8 2.8 multiply_add_fusion
  579.3 65.5 %while.33 = (s32[]{:T(128)}, f32[8,512,64]{1,2,0:T(8,128)}, f32[8,512,64]{1,2,0:T(8,128)}, f32[8,512,64]{1,2,0:T(8,128)}, bf16[8,512,64]{2,1,0:T(8,128)(2,1)}, /...) while((s32[]{:T(128)}, f32[8,512,64]{1,2,0:T(8,128)}, ...), condition=%wide.region_17.18_spmd.clone.clone, body=%wide.region_15.17_spmd.clone.sunk.clone | while | flops 170982912 | bytes 8996457 | solution.py:232
  662.2 5.2 convolution_convert_fusion.3
  667.5 8.0 convolution_convert_fusion.2
  675.5 8.1 convolution_convert_fusion.1
  683.9 7.9 convolution_convert_fusion
  696.3 7.3 all-to-all-start.2
  703.5 10.4 all-reduce.11.cloned.1.call-done
  713.9 2.9 fusion.41
  721.0 7.3 all-to-all-start.4
  728.3 3.8 sort.47
  733.4 61.5 %reduce-scatter.13.cloned.1.call-done = bf16[64,64]{1,0:T(8,128)(2,1)} async-done(((bf16[2048,64]{1,0:T(8,128)(2,1)}), bf16[64,64]{1,0:T(8,128)(2,1)}) %reduce-scatter.13.cloned.1.call-update) | async-done | bytes 8208 | tf_op jit(solution)/shard_map/reduce_scatter | solution.py:269
  796.2 78.5 %reduce-scatter.15.cloned.1.call-done = bf16[64,64]{1,0:T(8,128)(2,1)} async-done(((bf16[2048,64]{1,0:T(8,128)(2,1)}), bf16[64,64]{1,0:T(8,128)(2,1)}) %reduce-scatter.15.cloned.1.call-update) | async-done | bytes 8208 | tf_op jit(solution)/shard_map/reduce_scatter | solution.py:272
  878.7 64.4 %all-reduce.2 = (bf16[2048]{0:T(1024)(128)(2,1)S(1)}, bf16[2048]{0:T(1024)(128)(2,1)S(1)}) all-reduce(bf16[2048]{0:T(1024)(128)(2,1)S(1)} %get-tuple-element.249, bf16[2048]{0:T(1024)(128)(2,1)S(1)} %copy-done.20), channel_id=5, replica_groups=mesh['row'=32,'col'=4] {'row'}, use_global_device_ids=true, to_apply=%region_23.24.clone | all-reduce | flops 4096 | bytes 16384
  946.4 10.0 reduce-scatter.11.cloned.1.call-done
  957.9 80.2 %reduce-scatter.17.cloned.1.call-done = bf16[64,512]{1,0:T(8,128)(2,1)} async-done(((bf16[2048,512]{1,0:T(8,128)(2,1)}), bf16[64,512]{1,0:T(8,128)(2,1)}) %reduce-scatter.17.cloned.1.call-update) | async-done | bytes 65552 | tf_op jit(solution)/shard_map/reduce_scatter | solution.py:275
  1039.6 86.9 %reduce-scatter.19.cloned.1.call-done = bf16[64,1408]{1,0:T(8,128)(2,1)} async-done(((bf16[2048,1408]{1,0:T(8,128)(2,1)}), bf16[64,1408]{1,0:T(8,128)(2,1)}) %reduce-scatter.19.cloned.1.call-update) | async-done | bytes 180240 | tf_op jit(solution)/shard_map/reduce_scatter | solution.py:210
  1128.2 87.2 %reduce-scatter.21.cloned.1.call-done = bf16[64,1408]{1,0:T(8,128)(2,1)} async-done(((bf16[2048,1408]{1,0:T(8,128)(2,1)}), bf16[64,1408]{1,0:T(8,128)(2,1)}) %reduce-scatter.21.cloned.1.call-update) | async-done | bytes 180240 | tf_op jit(solution)/shard_map/reduce_scatter | solution.py:213
  1217.0 86.7 %reduce-scatter.23.cloned.1.call-done = bf16[64,1408]{1,0:T(8,128)(2,1)} async-done(((bf16[2048,1408]{1,0:T(8,128)(2,1)}), bf16[64,1408]{1,0:T(8,128)(2,1)}) %reduce-scatter.23.cloned.1.call-update) | async-done | bytes 180240 | tf_op jit(solution)/shard_map/reduce_scatter | solution.py:216
  (282 shorter events, 169.7 us)
Async XLA Ops:
  7.2 17.9 %copy-start = (bf16[512,512]{1,0:T(8,128)(2,1)S(1)}, bf16[512,512]{1,0:T(8,128)(2,1)}, u32[]{:S(2)}) copy-start(bf16[512,512]{1,0:T(8,128)(2,1)} %param.17) | copy-start | bytes 1572868
  12.3 24.0 %copy-start.16 = (s32[1024]{0:T(1024)}, s32[1024]{0:T(1024)S(1)}, u32[]{:S(2)}) copy-start(s32[1024]{0:T(1024)S(1)} %pad_clamp_fusion.3) | copy-start | bytes 12292
  16.6 15.7 %all-to-all-start.1 = ((s32[32,16,1]{1,2,0:T(1,128)}), s32[32,16,1]{1,2,0:T(1,128)S(1)}, u32[]{:S(2)}, u32[]{:S(2)}) async-start(s32[32,16,1]{1,2,0:T(1,128)} %bitcast.2), calls=%async_computation.1 | async-start | bytes 32768 | tf_op jit(solution)/shard_map/all_to_all | solution.py:121
  27.7 24.6 %copy-start.26 = (s32[512]{0:T(512)S(1)}, s32[512]{0:T(512)}, u32[]{:S(2)}) copy-start(s32[512]{0:T(512)} %param.20) | copy-start | bytes 6148
  27.7 25.3 %copy-start.22 = (bf16[64,64]{1,0:T(8,128)(2,1)S(1)}, bf16[64,64]{1,0:T(8,128)(2,1)}, u32[]{:S(2)}) copy-start(bf16[64,64]{1,0:T(8,128)(2,1)} %param.23) | copy-start | bytes 24580
  27.7 47.8 %copy-start.23 = (bf16[64,64]{1,0:T(8,128)(2,1)S(1)}, bf16[64,64]{1,0:T(8,128)(2,1)}, u32[]{:S(2)}) copy-start(bf16[64,64]{1,0:T(8,128)(2,1)} %param.24) | copy-start | bytes 24580
  32.3 15.7 %all-to-all-start = ((bf16[32,16,512]{2,1,0:T(8,128)(2,1)}), bf16[32,16,512]{2,1,0:T(8,128)(2,1)S(1)}, u32[]{:S(2)}, u32[]{:S(2)}) async-start(bf16[32,16,512]{2,1,0:T(8,128)(2,1)} %bitcast), calls=%async_computation | async-start | bytes 1048576 | tf_op jit(solution)/shard_map/all_to_all | solution.py:119
  36.2 66.3 %all-gather.20.cloned.1.call-start = ((), (), s32[]{:S(2)}) async-start(), calls=%async_computation.29 | async-start | bytes 2621440 | tf_op jit(solution)/shard_map/all_gather | solution.py:125
  41.3 11.6 copy-start.21
  48.0 56.8 %copy-start.24 = (f32[2048]{0:T(1024)S(1)}, f32[2048]{0:T(1024)}, u32[]{:S(2)}) copy-start(f32[2048]{0:T(1024)} %param.21) | copy-start | bytes 24580
  50.6 75.0 %all-gather.10.cloned.1.call-start = ((), (), s32[]{:S(2)}) async-start(), calls=%async_computation.13 | async-start | bytes 2162688 | tf_op jit(solution)/shard_map/all_gather | solution.py:129
  51.4 119.8 %all-gather.12.cloned.1.call-start = ((), (), s32[]{:S(2)}) async-start(), calls=%async_computation.14 | async-start | bytes 2162688 | tf_op jit(solution)/shard_map/all_gather | solution.py:132
  52.1 216.2 %all-reduce.7.cloned.1.call-start = ((), (), s32[]{:S(2)}) async-start(), calls=%async_computation.15 | async-start | bytes 8388608 | tf_op jit(solution)/shard_map/psum | solution.py:173
  52.2 55.4 %copy-start.29 = (f32[32]{0:T(128)}, f32[32]{0:T(128)S(1)}, u32[]{:S(2)}) copy-start(f32[32]{0:T(128)S(1)} %negate_power_fusion) | copy-start | bytes 388
  53.0 54.5 %copy-start.15 = (f32[512]{0:T(512)}, f32[512]{0:T(512)S(1)}, u32[]{:S(2)}) copy-start(f32[512]{0:T(512)S(1)} %fusion.70) | copy-start | bytes 6148
  75.5 34.8 %copy-start.10 = (bf16[2048,64]{1,0:T(8,128)(2,1)}, bf16[2048,64]{1,0:T(8,128)(2,1)S(1)}, u32[]{:S(2)}) copy-start(bf16[2048,64]{1,0:T(8,128)(2,1)S(1)} %all_gather.36) | copy-start | bytes 786436
  102.5 5.2 copy-start.6
  104.8 2.8 copy-start.18
  153.4 22.7 %copy-start.9 = (bf16[8,512,64]{2,1,0:T(8,128)(2,1)}, bf16[8,512,64]{2,1,0:T(8,128)(2,1)S(1)}, u32[]{:S(2)}) copy-start(bf16[8,512,64]{2,1,0:T(8,128)(2,1)S(1)} %get-tuple-element.556) | copy-start | bytes 1572868
  176.1 142.8 %all-gather.14.cloned.1.call-start = ((), (), s32[]{:S(2)}) async-start(), calls=%async_computation.16 | async-start | bytes 5947392 | tf_op jit(solution)/shard_map/all_gather | solution.py:179
  176.7 192.1 %all-gather.16.cloned.1.call-start = ((), (), s32[]{:S(2)}) async-start(), calls=%async_computation.17 | async-start | bytes 5947392 | tf_op jit(solution)/shard_map/all_gather | solution.py:180
  177.3 223.6 %all-gather.22.cloned.1.call-start = ((), (), s32[]{:S(2)}) async-start(), calls=%async_computation.30 | async-start | bytes 2621440 | tf_op jit(solution)/shard_map/all_gather | solution.py:126
  180.0 88.3 %copy-start.7 = (bf16[512,2048]{1,0:T(8,128)(2,1)S(1)}, bf16[512,2048]{1,0:T(8,128)(2,1)}, u32[]{:S(2)}) copy-start(bf16[512,2048]{1,0:T(8,128)(2,1)} %all-gather.20.cloned.1.call-done) | copy-start | bytes 6291460
  199.9 252.1 %all-gather.18.cloned.1.call-start = ((), (), s32[]{:S(2)}) async-start(), calls=%async_computation.18 | async-start | bytes 5947392 | tf_op jit(solution)/shard_map/all_gather | solution.py:181
  200.6 72.4 %copy-start.14 = (f32[2048]{0:T(1024)S(1)}, f32[2048]{0:T(1024)}, u32[]{:S(2)}) copy-start(f32[2048]{0:T(1024)} %param.26) | copy-start | bytes 24580
  200.6 365.2 %all-reduce.9.cloned.1.call-start = ((), (), s32[]{:S(2)}) async-start(), calls=%async_computation.20 | async-start | bytes 8388608 | tf_op jit(solution)/shard_map/psum | solution.py:205
  462.3 6.6 copy-start.33
  462.3 6.6 copy-start.32
  462.3 6.6 copy-start.30
  474.0 218.0 %reduce-scatter.9.cloned.1.call-start = ((), (), s32[]{:S(2)}) async-start(), calls=%async_computation.19 | async-start | bytes 2621440 | tf_op jit(solution)/shard_map/reduce_scatter | solution.py:187
  482.1 231.8 %all-reduce.11.cloned.1.call-start = ((), (), s32[]{:S(2)}) async-start(), calls=%async_computation.21 | async-start | bytes 4194304 | tf_op jit(solution)/shard_map/psum | solution.py:261
  565.9 5.2 copy-start.3
  565.9 5.9 copy-start.8
  571.8 4.8 copy-start.12
  647.4 4.4 copy-start.11
  655.2 139.7 %reduce-scatter.13.cloned.1.call-start = ((), (), s32[]{:S(2)}) async-start(), calls=%async_computation.23 | async-start | bytes 540672 | tf_op jit(solution)/shard_map/reduce_scatter | solution.py:269
  657.1 217.6 %reduce-scatter.15.cloned.1.call-start = ((), (), s32[]{:S(2)}) async-start(), calls=%async_computation.24 | async-start | bytes 540672 | tf_op jit(solution)/shard_map/reduce_scatter | solution.py:272
  659.2 297.1 %reduce-scatter.11.cloned.1.call-start = ((), (), s32[]{:S(2)}) async-start(), calls=%async_computation.22 | async-start | bytes 2162688 | tf_op jit(solution)/shard_map/reduce_scatter | solution.py:266
  662.1 375.9 %reduce-scatter.17.cloned.1.call-start = ((), (), s32[]{:S(2)}) async-start(), calls=%async_computation.25 | async-start | bytes 2162688 | tf_op jit(solution)/shard_map/reduce_scatter | solution.py:275
  667.4 459.0 %reduce-scatter.19.cloned.1.call-start = ((), (), s32[]{:S(2)}) async-start(), calls=%async_computation.26 | async-start | bytes 5947392 | tf_op jit(solution)/shard_map/reduce_scatter | solution.py:210
  675.5 539.8 %reduce-scatter.21.cloned.1.call-start = ((), (), s32[]{:S(2)}) async-start(), calls=%async_computation.27 | async-start | bytes 5947392 | tf_op jit(solution)/shard_map/reduce_scatter | solution.py:213
  683.6 620.1 %reduce-scatter.23.cloned.1.call-start = ((), (), s32[]{:S(2)}) async-start(), calls=%async_computation.28 | async-start | bytes 5947392 | tf_op jit(solution)/shard_map/reduce_scatter | solution.py:216
  696.3 24.8 %all-to-all-start.2 = ((bf16[32,16,512]{2,1,0:T(8,128)(2,1)}), bf16[32,16,512]{2,1,0:T(8,128)(2,1)S(1)}, u32[]{:S(2)}, u32[]{:S(2)}) async-start(bf16[32,16,512]{2,1,0:T(8,128)(2,1)} %bitcast.14), calls=%async_computation.3 | async-start | bytes 1048576 | tf_op jit(solution)/shard_map/all_to_all | solution.py:283
  716.8 11.5 copy-start.28
  716.9 15.3 %copy-start.31 = (u32[128]{0:T(128)S(1)}, u32[128]{0:T(128)}, u32[]{:S(2)}) copy-start(u32[128]{0:T(128)} %constant.120) | copy-start | bytes 1540
  718.4 160.3 %copy-start.20 = (bf16[2048]{0:T(1024)(128)(2,1)S(1)}, bf16[2048]{0:T(1024)(128)(2,1)}, u32[]{:S(2)}) copy-start(bf16[2048]{0:T(1024)(128)(2,1)} %get-tuple-element.247) | copy-start | bytes 12292
  721.0 222.7 %all-to-all-start.4 = ((bf16[32,16,512]{2,1,0:T(8,128)(2,1)}), bf16[32,16,512]{2,1,0:T(8,128)(2,1)S(1)}, u32[]{:S(2)}, u32[]{:S(2)}) async-start(bf16[32,16,512]{2,1,0:T(8,128)(2,1)} %bitcast.24), calls=%async_computation.5 | async-start | bytes 1048576 | tf_op jit(solution)/shard_map/all_to_all | solution.py:284
  876.1 429.3 %copy-start.1 = (bf16[512,512]{1,0:T(8,128)(2,1)S(1)}, bf16[512,512]{1,0:T(8,128)(2,1)}, u32[]{:S(2)}) copy-start(bf16[512,512]{1,0:T(8,128)(2,1)} %param.17) | copy-start | bytes 1572868
  (8 other events, 12.7 us)
Sparse Core Ops, SparseCore 0:
  50.7 28.4 all-gather.19
  81.5 44.0 all-gather.9
  127.9 43.2 all-gather.11
  176.2 91.9 all-reduce.6
  270.6 48.3 all-gather.13
  321.3 47.4 all-gather.15
  371.1 29.7 all-gather.21
  403.4 48.4 all-gather.17
  474.1 91.7 all-reduce.8
  568.1 29.5 reduce-scatter.8
  655.3 58.5 all-reduce.10
  717.8 77.0 reduce-scatter.12
  798.4 76.3 reduce-scatter.14
  878.2 78.1 reduce-scatter.10
  959.8 78.2 reduce-scatter.16
  1041.7 84.7 reduce-scatter.18
  1130.5 84.7 reduce-scatter.20
  1218.9 84.7 reduce-scatter.22
where the time goes:
time: 1320 us; the launch traced here: 1310 us
  waiting for transfers between devices  860 us (65%)
  matrix products  170 us (13%)
  blocking collectives  131 us (10%)
  other arithmetic  55.9 us (4%)
  local copies, waits for them, and re-layouts  51.2 us (4%)
  starting transfers between devices  28.6 us (2%)
  between operations  16 us (1%)
    dot_general x77, matrix products, matmul(): return jnp.dot(left, right, preferred_element_type=jnp.float32)  170 us
    reduce_scatter x1, waiting for transfers between devices, body(): lax.psum_scatter(up_weight_grad.astype(jnp.bfloat16), 'row', scatter_dime...  87.2 us
    reduce_scatter x1, waiting for transfers between devices, body(): lax.psum_scatter(gate_weight_grad.astype(jnp.bfloat16), 'row', scatter_di...  86.9 us
    reduce_scatter x1, waiting for transfers between devices, body(): lax.psum_scatter(down_weight_grad.astype(jnp.bfloat16), 'row', scatter_di...  86.7 us
    psum x1, waiting for transfers between devices, body(): normed_grad_two = lax.psum(normed_terms_two, 'col')  83.7 us
    reduce_scatter x1, waiting for transfers between devices, body(): lax.psum_scatter(output_weight_grad.astype(jnp.bfloat16), 'row', scatter_...  80.2 us
    reduce_scatter x1, waiting for transfers between devices, body(): lax.psum_scatter(value_weight_grad.astype(jnp.bfloat16), 'row', scatter_d...  78.5 us
    psum x1, waiting for transfers between devices, body(): attn_full = lax.psum(attn_terms, 'col')  67.2 us
  transfers between devices with their start and end apart: 22, of which 18 were waited for; matrix products, arithmetic and copies ran while one was open for 18% of the time, Pallas kernels for 0%

commit v1 on v0

--- a/solution.py
+++ b/solution.py
@@ -9,6 +9,12 @@
 HD = 64
 EPS = 1e-05
 ROPE_BASE = 10000.0
+
+
+def add_all(x, axis):
+    parts = lax.all_gather(x, axis, axis=0, tiled=False)
+    acc = parts.sum(axis=0)
+    return acc
 
 
 def rope_tables(positions):
@@ -170,7 +176,7 @@
         .astype(jnp.bfloat16)
     )
     attn_terms = matmul(mixed, output_w.T)
-    attn_full = lax.psum(attn_terms, "col")
+    attn_full = add_all(attn_terms, "col")
     resid = rows_wide + attn_full
     inv_two = rms_scale(resid)
     normed_two = (resid * inv_two * ffn_gain).astype(jnp.bfloat16)

time: 1320 us -> 1380 us (1.045)
  waiting for transfers between devices: 860 us -> 914 us
    all_gather x0 -> x1, waiting for transfers between devices: none -> 130 us  [add_all(): parts = lax.all_gather(x, axis, axis=0, tiled=False)]
    psum x1 -> x0, waiting for transfers between devices: 67.2 us -> none  [body(): attn_full = lax.psum(attn_terms, 'col')]
where the time goes in v1:
time: 1380 us
  waiting for transfers between devices  914 us (66%)
  matrix products  171 us (12%)
  blocking collectives  130 us (9%)
  other arithmetic  66.4 us (5%)
  local copies, waits for them, and re-layouts  50.4 us (4%)
  starting transfers between devices  28.2 us (2%)
  between operations  15.8 us (1%)
    dot_general x77, matrix products, matmul(): return jnp.dot(left, right, preferred_element_type=jnp.float32)  171 us
    all_gather x1, waiting for transfers between devices, add_all(): parts = lax.all_gather(x, axis, axis=0, tiled=False)  130 us
    reduce_scatter x1, waiting for transfers between devices, body(): lax.psum_scatter(gate_weight_grad.astype(jnp.bfloat16), 'row', scatter_di...  87.4 us
    reduce_scatter x1, waiting for transfers between devices, body(): lax.psum_scatter(down_weight_grad.astype(jnp.bfloat16), 'row', scatter_di...  87.1 us
    reduce_scatter x1, waiting for transfers between devices, body(): lax.psum_scatter(up_weight_grad.astype(jnp.bfloat16), 'row', scatter_dime...  86.6 us
    psum x1, waiting for transfers between devices, body(): normed_grad_two = lax.psum(normed_terms_two, 'col')  83.9 us
    reduce_scatter x1, waiting for transfers between devices, body(): lax.psum_scatter(output_weight_grad.astype(jnp.bfloat16), 'row', scatter_...  80.6 us
    reduce_scatter x1, waiting for transfers between devices, body(): lax.psum_scatter(value_weight_grad.astype(jnp.bfloat16), 'row', scatter_d...  78.9 us
  transfers between devices with their start and end apart: 22, of which 18 were waited for; matrix products, arithmetic and copies ran while one was open for 18% of the time, Pallas kernels for 0%

profile of v1, /device:TPU:0, one launch (start us, length us, event | category | flops | bytes accessed | tf_op | source)
XLA Modules:
  0.0 1376.3 jit_solution(3324863743826475022)
XLA Ops:
  7.2 4.5 sort.45
  12.3 3.6 gather_fusion.1
  16.6 8.4 all-to-all-start.1
  27.7 4.6 all-to-all-done.1
  32.3 3.9 all-to-all-start
  37.5 3.8 sort.46
  41.3 6.6 all-to-all-done
  53.0 22.4 %all_gather.42 = bf16[2048,64]{1,0:T(8,128)(2,1)S(1)} all-gather(bf16[64,64]{1,0:T(8,128)(2,1)S(1)} %copy-done.23), channel_id=1, replica_groups=mesh['row'=32,'col'=4] {'row'}, dimensions={0}, use_global_device_ids=true | all-gather | bytes 270336 | tf_op jit(solution)/shard_map/all_gather | solution.py:136
  75.5 26.7 %all_gather.43 = bf16[2048,64]{1,0:T(8,128)(2,1)} all-gather(bf16[64,64]{1,0:T(8,128)(2,1)S(1)} %copy-done.24), channel_id=1, replica_groups=mesh['row'=32,'col'=4] {'row'}, dimensions={0}, use_global_device_ids=true | all-gather | bytes 270336 | tf_op jit(solution)/shard_map/all_gather | solution.py:137
  111.2 14.5 %all-gather.12.cloned.1.call-done = bf16[2048,512]{1,0:T(8,128)(2,1)} async-done(((bf16[64,512]{1,0:T(8,128)(2,1)}), bf16[2048,512]{1,0:T(8,128)(2,1)}) %all-gather.12.cloned.1.call-update) | async-done | bytes 2097168 | tf_op jit(solution)/shard_map/all_gather | solution.py:135
  125.6 3.0 fusion.73
  129.4 24.0 %while.32 = (s32[]{:T(128)}, bf16[8,512,64]{1,2,0:T(8,128)(2,1)S(1)}, f32[8,512]{1,0:T(8,128)}, bf16[8,512,64]{2,1,0:T(8,128)(2,1)S(1)}, bf16[1,512,64]{2,1,0:T(...) while((s32[]{:T(128)}, bf16[8,512,64]{1,2,0:T(8,128)(2,1)S(1)}, ...), condition=%wide.region_8.9_spmd.clone.clone, body=%wide.region_5.8_spmd.clone.sunk.clone | while | flops 69991936 | bytes 3695189 | solution.py:163
  153.4 17.8 %all-gather.14.cloned.1.call-done = bf16[2048,512]{1,0:T(8,128)(2,1)} async-done(((bf16[64,512]{1,0:T(8,128)(2,1)}), bf16[2048,512]{1,0:T(8,128)(2,1)}) %all-gather.14.cloned.1.call-update) | async-done | bytes 2097168 | tf_op jit(solution)/shard_map/all_gather | solution.py:138
  171.2 4.9 fusion.75
  179.4 16.8 %all_to_all.60 = bf16[32,16,512]{2,1,0:T(8,128)(2,1)S(1)} all-to-all(bf16[32,16,512]{2,1,0:T(8,128)(2,1)S(1)} %bitcast.197), channel_id=1, replica_groups=mesh['row'=32,'col'=4] {'row'}, dimensions={0} | all-to-all | bytes 1048576 | tf_op jit(solution)/shard_map/all_to_all | solution.py:126
  199.8 129.8 %all-gather.24.cloned.1.call-done = f32[2048,2048]{1,0:T(8,128)} async-done(((f32[512,2048]{1,0:T(8,128)}), f32[2048,2048]{1,0:T(8,128)}) %all-gather.24.cloned.1.call-update) | async-done | bytes 16777232 | tf_op jit(solution)/shard_map/all_gather | solution.py:15
  329.6 10.4 reduce_sum.102
  346.7 34.4 %all-gather.16.cloned.1.call-done = bf16[2048,1408]{1,0:T(8,128)(2,1)} async-done(((bf16[64,1408]{1,0:T(8,128)(2,1)}), bf16[2048,1408]{1,0:T(8,128)(2,1)}) %all-gather.16.cloned.1.call-update) | async-done | bytes 5767184 | tf_op jit(solution)/shard_map/all_gather | solution.py:185
  381.2 8.3 fusion.76
  389.4 41.3 %all-gather.18.cloned.1.call-done = bf16[2048,1408]{1,0:T(8,128)(2,1)} async-done(((bf16[64,1408]{1,0:T(8,128)(2,1)}), bf16[2048,1408]{1,0:T(8,128)(2,1)}) %all-gather.18.cloned.1.call-update) | async-done | bytes 5767184 | tf_op jit(solution)/shard_map/all_gather | solution.py:186
  430.7 8.3 fusion.77
  439.1 23.7 %all-gather.26.cloned.1.call-done = bf16[512,2048]{1,0:T(8,128)(2,1)} async-done(((bf16[512,512]{1,0:T(8,128)(2,1)}), bf16[512,2048]{1,0:T(8,128)(2,1)}) %all-gather.26.cloned.1.call-update) | async-done | bytes 2097168 | tf_op jit(solution)/shard_map/all_gather | solution.py:132
  462.8 50.8 %all-gather.20.cloned.1.call-done = bf16[2048,1408]{1,0:T(8,128)(2,1)} async-done(((bf16[64,1408]{1,0:T(8,128)(2,1)}), bf16[2048,1408]{1,0:T(8,128)(2,1)}) %all-gather.20.cloned.1.call-update) | async-done | bytes 5767184 | tf_op jit(solution)/shard_map/all_gather | solution.py:187
  513.6 10.3 multiply_convert_fusion.3
  523.9 7.1 fusion.78
  531.0 5.0 convolution_add_fusion
  536.1 7.8 convolution_convert_fusion.5
  544.1 83.9 %all-reduce.6.cloned.1.call-done = f32[512,2048]{1,0:T(8,128)} async-done(((f32[512,2048]{1,0:T(8,128)}), f32[512,2048]{1,0:T(8,128)}) %all-reduce.6.cloned.1.call-update) | async-done | bytes 4194320 | tf_op jit(solution)/shard_map/psum | solution.py:211
  627.9 5.2 multiply_reduce_fusion.1
  641.3 65.5 %while.33 = (s32[]{:T(128)}, f32[8,512,64]{1,2,0:T(8,128)}, f32[8,512,64]{1,2,0:T(8,128)}, f32[8,512,64]{1,2,0:T(8,128)}, bf16[8,512,64]{2,1,0:T(8,128)(2,1)}, /...) while((s32[]{:T(128)}, f32[8,512,64]{1,2,0:T(8,128)}, ...), condition=%wide.region_17.18_spmd.clone.clone, body=%wide.region_15.17_spmd.clone.sunk.clone | while | flops 170982912 | bytes 8996457 | solution.py:238
  721.2 2.9 convolution_convert_fusion.4
  724.2 5.3 convolution_convert_fusion.3
  729.7 8.0 convolution_convert_fusion.2
  737.8 8.1 convolution_convert_fusion.1
  745.9 7.9 convolution_convert_fusion
  758.3 7.5 all-to-all-start.2
  765.8 10.2 all-reduce.8.cloned.1.call-done
  776.0 2.9 fusion.41
  783.1 7.3 all-to-all-start.4
  790.4 3.8 sort.47
  795.4 61.9 %reduce-scatter.13.cloned.1.call-done = bf16[64,64]{1,0:T(8,128)(2,1)} async-done(((bf16[2048,64]{1,0:T(8,128)(2,1)}), bf16[64,64]{1,0:T(8,128)(2,1)}) %reduce-scatter.13.cloned.1.call-update) | async-done | bytes 8208 | tf_op jit(solution)/shard_map/reduce_scatter | solution.py:275
  858.7 78.9 %reduce-scatter.15.cloned.1.call-done = bf16[64,64]{1,0:T(8,128)(2,1)} async-done(((bf16[2048,64]{1,0:T(8,128)(2,1)}), bf16[64,64]{1,0:T(8,128)(2,1)}) %reduce-scatter.15.cloned.1.call-update) | async-done | bytes 8208 | tf_op jit(solution)/shard_map/reduce_scatter | solution.py:278
  941.5 64.4 %all-reduce.2 = (bf16[2048]{0:T(1024)(128)(2,1)S(1)}, bf16[2048]{0:T(1024)(128)(2,1)S(1)}) all-reduce(bf16[2048]{0:T(1024)(128)(2,1)S(1)} %get-tuple-element.249, bf16[2048]{0:T(1024)(128)(2,1)S(1)} %copy-done.20), channel_id=6, replica_groups=mesh['row'=32,'col'=4] {'row'}, use_global_device_ids=true, to_apply=%region_23.24.clone | all-reduce | flops 4096 | bytes 16384
  1009.1 10.4 reduce-scatter.11.cloned.1.call-done
  1021.0 80.6 %reduce-scatter.17.cloned.1.call-done = bf16[64,512]{1,0:T(8,128)(2,1)} async-done(((bf16[2048,512]{1,0:T(8,128)(2,1)}), bf16[64,512]{1,0:T(8,128)(2,1)}) %reduce-scatter.17.cloned.1.call-update) | async-done | bytes 65552 | tf_op jit(solution)/shard_map/reduce_scatter | solution.py:281
  1103.1 87.4 %reduce-scatter.19.cloned.1.call-done = bf16[64,1408]{1,0:T(8,128)(2,1)} async-done(((bf16[2048,1408]{1,0:T(8,128)(2,1)}), bf16[64,1408]{1,0:T(8,128)(2,1)}) %reduce-scatter.19.cloned.1.call-update) | async-done | bytes 180240 | tf_op jit(solution)/shard_map/reduce_scatter | solution.py:216
  1192.2 86.6 %reduce-scatter.21.cloned.1.call-done = bf16[64,1408]{1,0:T(8,128)(2,1)} async-done(((bf16[2048,1408]{1,0:T(8,128)(2,1)}), bf16[64,1408]{1,0:T(8,128)(2,1)}) %reduce-scatter.21.cloned.1.call-update) | async-done | bytes 180240 | tf_op jit(solution)/shard_map/reduce_scatter | solution.py:219
  1280.4 87.1 %reduce-scatter.23.cloned.1.call-done = bf16[64,1408]{1,0:T(8,128)(2,1)} async-done(((bf16[2048,1408]{1,0:T(8,128)(2,1)}), bf16[64,1408]{1,0:T(8,128)(2,1)}) %reduce-scatter.23.cloned.1.call-update) | async-done | bytes 180240 | tf_op jit(solution)/shard_map/reduce_scatter | solution.py:222
  (285 shorter events, 171.2 us)
Async XLA Ops:
  7.2 17.9 %copy-start = (bf16[512,512]{1,0:T(8,128)(2,1)S(1)}, bf16[512,512]{1,0:T(8,128)(2,1)}, u32[]{:S(2)}) copy-start(bf16[512,512]{1,0:T(8,128)(2,1)} %param.17) | copy-start | bytes 1572868
  12.3 38.3 %copy-start.16 = (s32[1024]{0:T(1024)}, s32[1024]{0:T(1024)S(1)}, u32[]{:S(2)}) copy-start(s32[1024]{0:T(1024)S(1)} %pad_clamp_fusion.3) | copy-start | bytes 12292
  16.6 15.7 %all-to-all-start.1 = ((s32[32,16,1]{1,2,0:T(1,128)}), s32[32,16,1]{1,2,0:T(1,128)S(1)}, u32[]{:S(2)}, u32[]{:S(2)}) async-start(s32[32,16,1]{1,2,0:T(1,128)} %bitcast.2), calls=%async_computation.1 | async-start | bytes 32768 | tf_op jit(solution)/shard_map/all_to_all | solution.py:127
  27.7 24.6 %copy-start.27 = (s32[512]{0:T(512)S(1)}, s32[512]{0:T(512)}, u32[]{:S(2)}) copy-start(s32[512]{0:T(512)} %param.20) | copy-start | bytes 6148
  27.7 25.3 %copy-start.23 = (bf16[64,64]{1,0:T(8,128)(2,1)S(1)}, bf16[64,64]{1,0:T(8,128)(2,1)}, u32[]{:S(2)}) copy-start(bf16[64,64]{1,0:T(8,128)(2,1)} %param.23) | copy-start | bytes 24580
  27.7 47.8 %copy-start.24 = (bf16[64,64]{1,0:T(8,128)(2,1)S(1)}, bf16[64,64]{1,0:T(8,128)(2,1)}, u32[]{:S(2)}) copy-start(bf16[64,64]{1,0:T(8,128)(2,1)} %param.24) | copy-start | bytes 24580
  32.3 15.7 %all-to-all-start = ((bf16[32,16,512]{2,1,0:T(8,128)(2,1)}), bf16[32,16,512]{2,1,0:T(8,128)(2,1)S(1)}, u32[]{:S(2)}, u32[]{:S(2)}) async-start(bf16[32,16,512]{2,1,0:T(8,128)(2,1)} %bitcast), calls=%async_computation | async-start | bytes 1048576 | tf_op jit(solution)/shard_map/all_to_all | solution.py:125
  36.2 66.3 %all-gather.22.cloned.1.call-start = ((), (), s32[]{:S(2)}) async-start(), calls=%async_computation.28 | async-start | bytes 2621440 | tf_op jit(solution)/shard_map/all_gather | solution.py:131
  41.3 61.1 %copy-start.21 = (s32[1024]{0:T(1024)}, s32[1024]{0:T(1024)S(1)}, u32[]{:S(2)}) copy-start(s32[1024]{0:T(1024)S(1)} %pad_clamp_fusion.2) | copy-start | bytes 12292
  48.0 56.7 %copy-start.25 = (f32[2048]{0:T(1024)S(1)}, f32[2048]{0:T(1024)}, u32[]{:S(2)}) copy-start(f32[2048]{0:T(1024)} %param.21) | copy-start | bytes 24580
  50.6 75.0 %all-gather.12.cloned.1.call-start = ((), (), s32[]{:S(2)}) async-start(), calls=%async_computation.13 | async-start | bytes 2162688 | tf_op jit(solution)/shard_map/all_gather | solution.py:135
  51.4 119.8 %all-gather.14.cloned.1.call-start = ((), (), s32[]{:S(2)}) async-start(), calls=%async_computation.14 | async-start | bytes 2162688 | tf_op jit(solution)/shard_map/all_gather | solution.py:138
  52.1 277.5 %all-gather.24.cloned.1.call-start = ((), (), s32[]{:S(2)}) async-start(), calls=%async_computation.29 | async-start | bytes 20971520 | tf_op jit(solution)/shard_map/all_gather | solution.py:15
  52.2 55.3 %copy-start.30 = (f32[32]{0:T(128)}, f32[32]{0:T(128)S(1)}, u32[]{:S(2)}) copy-start(f32[32]{0:T(128)S(1)} %negate_power_fusion) | copy-start | bytes 388
  53.0 54.5 %copy-start.15 = (f32[512]{0:T(512)}, f32[512]{0:T(512)S(1)}, u32[]{:S(2)}) copy-start(f32[512]{0:T(512)S(1)} %fusion.70) | copy-start | bytes 6148
  75.5 34.8 %copy-start.10 = (bf16[2048,64]{1,0:T(8,128)(2,1)}, bf16[2048,64]{1,0:T(8,128)(2,1)S(1)}, u32[]{:S(2)}) copy-start(bf16[2048,64]{1,0:T(8,128)(2,1)S(1)} %all_gather.42) | copy-start | bytes 786436
  102.5 5.2 copy-start.6
  153.4 22.7 %copy-start.9 = (bf16[8,512,64]{2,1,0:T(8,128)(2,1)}, bf16[8,512,64]{2,1,0:T(8,128)(2,1)S(1)}, u32[]{:S(2)}) copy-start(bf16[8,512,64]{2,1,0:T(8,128)(2,1)S(1)} %get-tuple-element.556) | copy-start | bytes 1572868
  176.1 20.0 %copy-start.22 = (s32[1024]{0:T(1024)S(1)}, s32[1024]{0:T(1024)}, u32[]{:S(2)}) copy-start(s32[1024]{0:T(1024)} %copy-done.21) | copy-start | bytes 12292
  176.2 205.0 %all-gather.16.cloned.1.call-start = ((), (), s32[]{:S(2)}) async-start(), calls=%async_computation.15 | async-start | bytes 5947392 | tf_op jit(solution)/shard_map/all_gather | solution.py:185
  176.8 254.0 %all-gather.18.cloned.1.call-start = ((), (), s32[]{:S(2)}) async-start(), calls=%async_computation.16 | async-start | bytes 5947392 | tf_op jit(solution)/shard_map/all_gather | solution.py:186
  177.3 285.5 %all-gather.26.cloned.1.call-start = ((), (), s32[]{:S(2)}) async-start(), calls=%async_computation.30 | async-start | bytes 2621440 | tf_op jit(solution)/shard_map/all_gather | solution.py:132
  198.8 314.7 %all-gather.20.cloned.1.call-start = ((), (), s32[]{:S(2)}) async-start(), calls=%async_computation.17 | async-start | bytes 5947392 | tf_op jit(solution)/shard_map/all_gather | solution.py:187
  199.6 428.4 %all-reduce.6.cloned.1.call-start = ((), (), s32[]{:S(2)}) async-start(), calls=%async_computation.19 | async-start | bytes 8388608 | tf_op jit(solution)/shard_map/psum | solution.py:211
  329.6 10.4 copy-start.7
  340.0 4.9 copy-start.14
  523.9 7.1 copy-start.34
  523.9 7.1 copy-start.33
  523.9 7.2 copy-start.31
  536.1 217.9 %reduce-scatter.9.cloned.1.call-start = ((), (), s32[]{:S(2)}) async-start(), calls=%async_computation.18 | async-start | bytes 2621440 | tf_op jit(solution)/shard_map/reduce_scatter | solution.py:193
  544.0 232.0 %all-reduce.8.cloned.1.call-start = ((), (), s32[]{:S(2)}) async-start(), calls=%async_computation.20 | async-start | bytes 4194304 | tf_op jit(solution)/shard_map/psum | solution.py:267
  627.9 5.2 copy-start.3
  627.9 5.9 copy-start.8
  633.9 4.8 copy-start.12
  709.5 4.4 copy-start.11
  717.3 140.0 %reduce-scatter.13.cloned.1.call-start = ((), (), s32[]{:S(2)}) async-start(), calls=%async_computation.22 | async-start | bytes 540672 | tf_op jit(solution)/shard_map/reduce_scatter | solution.py:275
  719.3 218.3 %reduce-scatter.15.cloned.1.call-start = ((), (), s32[]{:S(2)}) async-start(), calls=%async_computation.23 | async-start | bytes 540672 | tf_op jit(solution)/shard_map/reduce_scatter | solution.py:278
  721.2 298.4 %reduce-scatter.11.cloned.1.call-start = ((), (), s32[]{:S(2)}) async-start(), calls=%async_computation.21 | async-start | bytes 2162688 | tf_op jit(solution)/shard_map/reduce_scatter | solution.py:272
  724.1 377.5 %reduce-scatter.17.cloned.1.call-start = ((), (), s32[]{:S(2)}) async-start(), calls=%async_computation.24 | async-start | bytes 2162688 | tf_op jit(solution)/shard_map/reduce_scatter | solution.py:281
  729.5 461.0 %reduce-scatter.19.cloned.1.call-start = ((), (), s32[]{:S(2)}) async-start(), calls=%async_computation.25 | async-start | bytes 5947392 | tf_op jit(solution)/shard_map/reduce_scatter | solution.py:216
  737.7 541.0 %reduce-scatter.21.cloned.1.call-start = ((), (), s32[]{:S(2)}) async-start(), calls=%async_computation.26 | async-start | bytes 5947392 | tf_op jit(solution)/shard_map/reduce_scatter | solution.py:219
  745.9 621.7 %reduce-scatter.23.cloned.1.call-start = ((), (), s32[]{:S(2)}) async-start(), calls=%async_computation.27 | async-start | bytes 5947392 | tf_op jit(solution)/shard_map/reduce_scatter | solution.py:222
  758.3 24.8 %all-to-all-start.2 = ((bf16[32,16,512]{2,1,0:T(8,128)(2,1)}), bf16[32,16,512]{2,1,0:T(8,128)(2,1)S(1)}, u32[]{:S(2)}, u32[]{:S(2)}) async-start(bf16[32,16,512]{2,1,0:T(8,128)(2,1)} %bitcast.196), calls=%async_computation.3 | async-start | bytes 1048576 | tf_op jit(solution)/shard_map/all_to_all | solution.py:289
  778.9 11.5 copy-start.29
  778.9 15.2 %copy-start.32 = (u32[128]{0:T(128)S(1)}, u32[128]{0:T(128)}, u32[]{:S(2)}) copy-start(u32[128]{0:T(128)} %constant.120) | copy-start | bytes 1540
  780.5 161.0 %copy-start.20 = (bf16[2048]{0:T(1024)(128)(2,1)S(1)}, bf16[2048]{0:T(1024)(128)(2,1)}, u32[]{:S(2)}) copy-start(bf16[2048]{0:T(1024)(128)(2,1)} %get-tuple-element.247) | copy-start | bytes 12292
  783.1 223.4 %all-to-all-start.4 = ((bf16[32,16,512]{2,1,0:T(8,128)(2,1)}), bf16[32,16,512]{2,1,0:T(8,128)(2,1)S(1)}, u32[]{:S(2)}, u32[]{:S(2)}) async-start(bf16[32,16,512]{2,1,0:T(8,128)(2,1)} %bitcast.25), calls=%async_computation.5 | async-start | bytes 1048576 | tf_op jit(solution)/shard_map/all_to_all | solution.py:290
  938.9 430.3 %copy-start.1 = (bf16[512,512]{1,0:T(8,128)(2,1)S(1)}, bf16[512,512]{1,0:T(8,128)(2,1)}, u32[]{:S(2)}) copy-start(bf16[512,512]{1,0:T(8,128)(2,1)} %param.17) | copy-start | bytes 1572868
  (9 other events, 15.7 us)
Sparse Core Ops, SparseCore 0:
  50.7 28.4 all-gather.21
  81.5 44.0 all-gather.11
  127.9 43.2 all-gather.13
  176.3 153.2 all-gather.23
  331.7 49.4 all-gather.15
  383.3 47.4 all-gather.17
  433.0 29.7 all-gather.25
  465.0 48.4 all-gather.19
  536.2 91.7 all-reduce.5
  630.3 29.4 reduce-scatter.8
  717.5 58.4 all-reduce.7
  780.3 77.0 reduce-scatter.12
  861.2 76.3 reduce-scatter.14
  941.3 78.1 reduce-scatter.10
  1023.3 78.2 reduce-scatter.16
  1105.7 84.7 reduce-scatter.18
  1194.1 84.6 reduce-scatter.20
  1282.8 84.6 reduce-scatter.22
